TPU v7x, 256 devices: a whole 4x4x8 slice. The times are simulated.
256 devices in a mesh: gx: 16 (over x_hi, z), gz: 16 (over x_lo, y, core).
Axes of the slice: x: 4 (x_hi: 2, x_lo: 2; x = x_hi * 2 + x_lo), y: 4, z: 8, core: 2. Of those that a mesh axis runs over, the one named last changes fastest.
Arguments:
- direct_modes: bfloat16 [3, 256, 1024, 128], P(None, 'gx', 'gz'), may hold values from -6 to 6
- adjoint_modes: bfloat16 [3, 256, 1024, 128], P(None, 'gx', 'gz'), may hold values from -0.0048828125 to 0.0048828125
- stencil_taps: float32 [36, 256, 1024], P(None, 'gx', 'gz'), may hold values from -0.72 to 0.72
- coupling: float32 [18, 256, 1024], P(None, 'gx', 'gz'), may hold values from -1.2 to 1.2
Outputs:
- evolved: bfloat16 [3, 256, 1024, 128], P(None, 'gx', 'gz')
- reduced: float32 [64, 64], P('gx')
All inputs are finite; a program needn't handle non-finite values.
Results may differ from a plain program's by a relative error of at most 0.0031.
Values sent between devices are 32-bit elements; how exact they have to be, the bound alone decides.
A program may use at most 64 MiB of HBM per device.

v0:
```python
import jax
import jax.numpy as jnp
from jax import lax
from jax.sharding import PartitionSpec as P

STEPS = 4


def with_halo(x, sides, width):
    for axis, dim in sides:
        peers, length = (lax.axis_size(axis), x.shape[dim])
        up = [(i, (i + 1) % peers) for i in range(peers)]
        down = [(j, i) for i, j in up]
        last = lax.slice_in_dim(x, length - width, length, axis=dim)
        leading = lax.slice_in_dim(x, 0, width, axis=dim)
        before = lax.ppermute(last, axis, up)
        after = lax.ppermute(leading, axis, down)
        x = jnp.concatenate([before, x, after], axis=dim)
    return x


def lane_weight(lower, first, second):
    return jnp.where(lower, first[:, :, None], second[:, :, None])


def advance(padded, tap_block, mix_block):
    width_x = padded.shape[1] - 2
    width_z = padded.shape[2] - 2
    lanes_all = padded.shape[3]
    half = lanes_all // 2
    lower = lax.broadcasted_iota(jnp.int32, (1, 1, lanes_all), 2) < half
    swapped = jnp.concatenate((padded[:, :, :, half:], padded[:, :, :, :half]), axis=3)
    own = padded[:, 1 : 1 + width_x, 1 : 1 + width_z, :]
    total = jnp.zeros((3, width_x, width_z, lanes_all), jnp.float32)
    for side_at in range(2):
        source = padded if side_at == 0 else swapped
        for tap_at in range(9):
            shift_x = tap_at // 3
            shift_z = tap_at % 3
            shifted = source[:, shift_x : shift_x + width_x, shift_z : shift_z + width_z, :]
            weight = lane_weight(
                lower, tap_block[side_at * 9 + tap_at], tap_block[18 + side_at * 9 + tap_at]
            )
            total = total + weight[None] * shifted
    mixed = []
    for comp_at in range(3):
        term = jnp.zeros((width_x, width_z, lanes_all), jnp.float32)
        for other_at in range(3):
            weight = lane_weight(
                lower, mix_block[comp_at * 3 + other_at], mix_block[9 + comp_at * 3 + other_at]
            )
            term = term + weight * own[other_at]
        mixed.append(term)
    return own + total + jnp.stack(mixed, axis=0)


def plane_product(adjoint_flat, evolved_flat):
    result = jnp.zeros((adjoint_flat.shape[2], evolved_flat.shape[2]), jnp.float32)
    for plane_at in range(2):
        result = result + lax.dot_general(
            adjoint_flat[:, plane_at, :],
            evolved_flat[:, plane_at, :],
            (((0,), (0,)), ((), ())),
            preferred_element_type=jnp.float32,
        )
    return result


def body(direct_modes, adjoint_modes, stencil_taps, coupling):
    state = direct_modes.astype(jnp.float32)
    modes = state.shape[3] // 2
    for step in range(STEPS):
        padded = with_halo(state, (("gx", 1), ("gz", 2)), 1)
        state = advance(padded, stencil_taps, coupling)
    evolved = state.astype(jnp.bfloat16)
    adjoint_flat = adjoint_modes.reshape(-1, 2, modes)
    evolved_flat = evolved.reshape(-1, 2, modes)
    partial_sum = plane_product(adjoint_flat, evolved_flat)
    spanned = lax.psum(partial_sum, "gz")
    reduced = lax.psum_scatter(spanned, "gx", scatter_dimension=0, tiled=True)
    return (evolved, reduced)


def solution(mesh):
    placed = (
        P(None, "gx", "gz", None),
        P(None, "gx", "gz", None),
        P(None, "gx", "gz"),
        P(None, "gx", "gz"),
    )
    return jax.shard_map(
        body,
        mesh=mesh,
        in_specs=placed,
        out_specs=(P(None, "gx", "gz", None), P("gx", None)),
        check_vma=False,
    )
```

profile of v0, /device:TPU:2, one launch (start us, length us, event | category | flops | bytes accessed | tf_op | source)
XLA Modules:
  0.0 267.7 jit_solution(13567518144057242414)
XLA Ops:
  2.2 7.4 %collective-permute-start.1 = (f32[3,1,64,128]{3,2,1,0:T(8,128)}, f32[3,1,64,128]{3,2,1,0:T(8,128)S(1)}, u32[]{:S(2)}, u32[]{:S(2)}) collective-permute-start(f32[3,1,64,128]{3,2,1,0:T(8,128)} %get-tuple-element.51), channel_id=1, source_target_pairs={{16,0},{32,16},{48,32},{64,48},{80,64},{96,80},{112,96},{128,112},... | collective-permute-start | bytes 294920 | tf_op jit(solution)/shard_map/ppermute | solution.py:17
  12.3 3.2 %reshape.117 = bf16[3072,2,64]{2,1,0:T(2,128)(2,1)S(1)} reshape(bf16[3,16,64,128]{3,2,1,0:T(8,128)(2,1)} %param.5) | data formatting | bytes 1572864 | tf_op jit(solution)/shard_map/reshape | solution.py:76
  15.7 3.5 %fusion.172 = (bf16[3072,1,64]{2,1,0:T(2,128)(2,1)}, bf16[3072,1,64]{2,1,0:T(2,128)(2,1)}) fusion(bf16[3072,2,64]{2,1,0:T(2,128)(2,1)S(1)} %reshape.117), kind=kLoop, calls=%fused_computation.399 | loop fusion | bytes 1572864 | tf_op jit(solution)/shard_map/slice | solution.py:61
  19.5 3.9 %broadcast_select_fusion.8 = (f32[16,64,128]{2,1,0:T(8,128)S(1)}, f32[16,64,128]{2,1,0:T(8,128)S(1)}, f32[16,64,128]{2,1,0:T(8,128)S(1)}, f32[16,64,128]{2,1,0:T...) fusion(f32[16,64]{1,0:T(8,128)S(1)} %copy-done.47, ...), kind=kLoop, calls=%fused_computation.316 | loop fusion | flops 1179648 | bytes 4792448 | tf_op jit(solution)/shard_map/jit(_where)/select_n | solution.py:23
  23.4 4.1 %broadcast_select_fusion.17 = (f32[16,64,128]{2,1,0:T(8,128)}, f32[16,64,128]{2,1,0:T(8,128)}, f32[16,64,128]{2,1,0:T(8,128)}, f32[16,64,128]{2,1,0:T(8,128)}, f...) fusion(f32[16,64]{1,0:T(8,128)S(1)} %get-tuple-element.71, ...), kind=kLoop, calls=%fused_computation.325 | loop fusion | flops 1179648 | bytes 4792448 | tf_op jit(solution)/shard_map/jit(_where)/select_n | solution.py:23
  35.8 4.1 %copy.18 = bf16[3072,1,64]{0,2,1:T(8,128)(2,1)} copy(bf16[3072,1,64]{2,1,0:T(2,128)(2,1)} %get-tuple-element.43) | data formatting | bytes 786432
  39.9 4.1 %copy.20 = bf16[3072,1,64]{0,2,1:T(8,128)(2,1)} copy(bf16[3072,1,64]{2,1,0:T(2,128)(2,1)} %get-tuple-element.42) | data formatting | bytes 786432
  49.4 6.4 %fusion.106 = f32[3,16,64,128]{3,2,1,0:T(8,128)S(1)} fusion(f32[3,16,64,128]{3,2,1,0:T(8,128)S(1)} %convert_element_type.6, f32[3,18,66,64]{3,2,1,0:T(8,128)S(1)} %get-tuple-element.15, f32[3,18,66,64]{3,2,1,0:T(8,128)S(1)} %get-tuple-element.14, f32[3,18,65,128]{3,2,1,0:T(8,128)S(1)} %get-tuple-element.29, ...), kind=kLoop, calls=%fused_computation.188 | loop fusion | flops 19660800 | bytes 25614336 | tf_op jit(solution)/shard_map/add | solution.py:54
  55.9 5.0 %collective-permute-start.5 = (f32[3,1,64,128]{3,2,1,0:T(8,128)S(1)}, f32[3,1,64,128]{3,2,1,0:T(8,128)S(1)}, u32[]{:S(2)}, u32[]{:S(2)}) collective-permute-start(f32[3,1,64,128]{3,2,1,0:T(8,128)S(1)} %get-tuple-element.49), channel_id=1, source_target_pairs={{16,0},{32,16},{48,32},{64,48},{80,64},{96,80},{112,96},{128,112},... | collective-permute-start | bytes 294920 | tf_op jit(solution)/shard_map/ppermute | solution.py:17
  63.1 6.0 %collective-permute-done.4 = f32[3,1,64,128]{3,2,1,0:T(8,128)S(1)} collective-permute-done((f32[3,1,64,128]{3,2,1,0:T(8,128)S(1)}, f32[3,1,64,128]{3,2,1,0:T(8,128)S(1)}, u32[]{:S(2)}, u32[]{:S(2)}) %collective-permute-start.4) | collective-permute-done | bytes 98336 | tf_op jit(solution)/shard_map/ppermute | solution.py:16
  69.1 3.1 %collective-permute-start.7 = (f32[3,18,1,128]{3,2,1,0:T(1,128)S(1)}, f32[3,18,1,128]{3,2,1,0:T(1,128)S(1)}, u32[]{:S(2)}, u32[]{:S(2)}) collective-permute-start(f32[3,18,1,128]{3,2,1,0:T(1,128)S(1)} %get-tuple-element.27), channel_id=1, source_target_pairs={{1,0},{2,1},{3,2},{4,3},{5,4},{6,5},{7,6},{8,7},{9,8},{10,9},{11,1... | collective-permute-start | bytes 82952 | tf_op jit(solution)/shard_map/ppermute | solution.py:17
  73.8 3.8 %collective-permute-done.6 = f32[3,18,1,128]{3,2,1,0:T(1,128)S(1)} collective-permute-done((f32[3,18,1,128]{3,2,1,0:T(1,128)S(1)}, f32[3,18,1,128]{3,2,1,0:T(1,128)S(1)}, u32[]{:S(2)}, u32[]{:S(2)}) %collective-permute-start.6) | collective-permute-done | bytes 27680 | tf_op jit(solution)/shard_map/ppermute | solution.py:16
  78.9 6.5 %fusion.72 = f32[3,16,64,128]{3,2,1,0:T(8,128)S(1)} fusion(f32[3,16,64,128]{3,2,1,0:T(8,128)S(1)} %fusion.106, f32[3,18,66,64]{3,2,1,0:T(8,128)S(1)} %get-tuple-element.13, f32[3,18,66,64]{3,2,1,0:T(8,128)S(1)} %get-tuple-element.12, f32[3,18,65,128]{3,2,1,0:T(8,128)S(1)} %get-tuple-element.25, f32[3,1,64,128]{3,2,1,0:T(8,128)S(1)} %collective-permute-done.5, ...), kind=kLoop, calls=%fused_computation.131 | loop fusion | flops 19660800 | bytes 25614336 | tf_op jit(solution)/shard_map/add | solution.py:54
  90.1 3.7 %collective-permute-done.8 = f32[3,1,64,128]{3,2,1,0:T(8,128)S(1)} collective-permute-done((f32[3,1,64,128]{3,2,1,0:T(8,128)S(1)}, f32[3,1,64,128]{3,2,1,0:T(8,128)S(1)}, u32[]{:S(2)}, u32[]{:S(2)}) %collective-permute-start.8) | collective-permute-done | bytes 98336 | tf_op jit(solution)/shard_map/ppermute | solution.py:16
  95.5 4.1 %collective-permute-done.10 = f32[3,18,1,128]{3,2,1,0:T(1,128)S(1)} collective-permute-done((f32[3,18,1,128]{3,2,1,0:T(1,128)S(1)}, f32[3,18,1,128]{3,2,1,0:T(1,128)S(1)}, u32[]{:S(2)}, u32[]{:S(2)}) %collective-permute-start.10) | collective-permute-done | bytes 27680 | tf_op jit(solution)/shard_map/ppermute | solution.py:16
  101.0 6.5 %fusion.38 = f32[3,16,64,128]{3,2,1,0:T(8,128)S(1)} fusion(f32[3,16,64,128]{3,2,1,0:T(8,128)S(1)} %fusion.72, f32[3,18,66,64]{3,2,1,0:T(8,128)S(1)} %get-tuple-element.11, f32[3,18,66,64]{3,2,1,0:T(8,128)S(1)} %get-tuple-element.10, f32[3,18,65,128]{3,2,1,0:T(8,128)S(1)} %get-tuple-element.21, f32[3,1,64,128]{3,2,1,0:T(8,128)S(1)} %collective-permute-done.9, ...), kind=kLoop, calls=%fused_computation.74 | loop fusion | flops 19660800 | bytes 25614336 | tf_op jit(solution)/shard_map/add | solution.py:54
  112.2 3.7 %collective-permute-done.12 = f32[3,1,64,128]{3,2,1,0:T(8,128)S(1)} collective-permute-done((f32[3,1,64,128]{3,2,1,0:T(8,128)S(1)}, f32[3,1,64,128]{3,2,1,0:T(8,128)S(1)}, u32[]{:S(2)}, u32[]{:S(2)}) %collective-permute-start.12) | collective-permute-done | bytes 98336 | tf_op jit(solution)/shard_map/ppermute | solution.py:16
  117.5 4.2 %collective-permute-done.14 = f32[3,18,1,128]{3,2,1,0:T(1,128)S(1)} collective-permute-done((f32[3,18,1,128]{3,2,1,0:T(1,128)S(1)}, f32[3,18,1,128]{3,2,1,0:T(1,128)S(1)}, u32[]{:S(2)}, u32[]{:S(2)}) %collective-permute-start.14) | collective-permute-done | bytes 27680 | tf_op jit(solution)/shard_map/ppermute | solution.py:16
  123.0 7.3 %fusion.4 = bf16[3,16,64,128]{3,2,1,0:T(8,128)(2,1)} fusion(f32[3,16,64,128]{3,2,1,0:T(8,128)S(1)} %fusion.38, f32[3,18,66,64]{3,2,1,0:T(8,128)S(1)} %get-tuple-element.9, f32[3,18,66,64]{3,2,1,0:T(8,128)S(1)} %get-tuple-element.8, f32[3,18,65,128]{3,2,1,0:T(8,128)S(1)} %get-tuple-element.17, f32[3,1,64,128]{3,2,1,0:T(8,128)S(1)} %collective-permute-done.13, ...), kind=kLoop, calls=%fused_computation.17 | loop fusion | flops 20054016 | bytes 24827904 | tf_op jit(solution)/shard_map/convert_element_type | solution.py:75
  130.3 3.2 %reshape.116 = bf16[3072,2,64]{2,1,0:T(2,128)(2,1)S(1)} reshape(bf16[3,16,64,128]{3,2,1,0:T(8,128)(2,1)} %fusion.4) | data formatting | bytes 1572864 | tf_op jit(solution)/shard_map/reshape | solution.py:77
  133.5 3.1 %fusion.171 = (bf16[3072,1,64]{2,1,0:T(2,128)(2,1)S(1)}, bf16[3072,1,64]{2,1,0:T(2,128)(2,1)}) fusion(bf16[3072,2,64]{2,1,0:T(2,128)(2,1)S(1)} %reshape.116), kind=kLoop, calls=%fused_computation.398 | loop fusion | bytes 1572864 | tf_op jit(solution)/shard_map/slice | solution.py:62
  136.6 3.5 %copy.17 = bf16[3072,1,64]{0,2,1:T(8,128)(2,1)S(1)} copy(bf16[3072,1,64]{2,1,0:T(2,128)(2,1)} %get-tuple-element.41) | data formatting | bytes 786432
  142.2 71.9 %all-reduce = f32[64,64]{0,1:T(8,128)S(1)} all-reduce(f32[64,64]{0,1:T(8,128)S(1)} %fusion.137), channel_id=2, replica_groups=mesh['gx'=16,'gz'=16] {'gx'}, use_global_device_ids=true, to_apply=%region_1.2.clone | all-reduce | flops 4096 | bytes 32768
  214.1 52.9 %psum.8 = f32[4,64]{0,1:T(8,128)S(1)} all-reduce(f32[4,64]{0,1:T(8,128)S(1)} %constant_dynamic-slice_fusion), channel_id=1, replica_groups=mesh['gx'=16,'gz'=16] {'gz'}, use_global_device_ids=true, to_apply=%region_0.1 | all-reduce | flops 256 | bytes 2048 | tf_op jit(solution)/shard_map/psum | solution.py:79
  (166 shorter events, 40.2 us)
Async XLA Ops:
  0.6 10.3 %copy-start.20 = (f32[36,16,64]{2,1,0:T(8,128)S(1)}, f32[36,16,64]{2,1,0:T(8,128)}, u32[]{:S(2)}) copy-start(f32[36,16,64]{2,1,0:T(8,128)} %param.6) | copy-start | bytes 442372
  2.2 10.1 %copy-start.21 = (f32[18,16,64]{2,1,0:T(8,128)S(1)}, f32[18,16,64]{2,1,0:T(8,128)}, u32[]{:S(2)}) copy-start(f32[18,16,64]{2,1,0:T(8,128)} %param.7) | copy-start | bytes 221188
  2.2 28.2 %collective-permute-start.1 = (f32[3,1,64,128]{3,2,1,0:T(8,128)}, f32[3,1,64,128]{3,2,1,0:T(8,128)S(1)}, u32[]{:S(2)}, u32[]{:S(2)}) collective-permute-start(f32[3,1,64,128]{3,2,1,0:T(8,128)} %get-tuple-element.51), channel_id=1, source_target_pairs={{16,0},{32,16},{48,32},{64,48},{80,64},{96,80},{112,96},{128,112},... | collective-permute-start | bytes 294920 | tf_op jit(solution)/shard_map/ppermute | solution.py:17
  9.6 20.8 %collective-permute-start = (f32[3,1,64,128]{3,2,1,0:T(8,128)}, f32[3,1,64,128]{3,2,1,0:T(8,128)S(1)}, u32[]{:S(2)}, u32[]{:S(2)}) collective-permute-start(f32[3,1,64,128]{3,2,1,0:T(8,128)} %get-tuple-element.50), channel_id=1, source_target_pairs={{0,16},{16,32},{32,48},{48,64},{64,80},{80,96},{96,112},{112,128},... | collective-permute-start | bytes 294920 | tf_op jit(solution)/shard_map/ppermute | solution.py:16
  19.4 4.0 %copy-start.22 = (f32[16,64]{1,0:T(8,128)S(1)}, f32[16,64]{1,0:T(8,128)}, u32[]{:S(2)}) copy-start(f32[16,64]{1,0:T(8,128)} %get-tuple-element.75) | copy-start | bytes 12292
  19.4 4.0 %copy-start.23 = (f32[16,64]{1,0:T(8,128)S(1)}, f32[16,64]{1,0:T(8,128)}, u32[]{:S(2)}) copy-start(f32[16,64]{1,0:T(8,128)} %get-tuple-element.76) | copy-start | bytes 12292
  19.4 4.0 %copy-start.24 = (f32[16,64]{1,0:T(8,128)S(1)}, f32[16,64]{1,0:T(8,128)}, u32[]{:S(2)}) copy-start(f32[16,64]{1,0:T(8,128)} %get-tuple-element.77) | copy-start | bytes 12292
  19.4 4.0 %copy-start.25 = (f32[16,64]{1,0:T(8,128)S(1)}, f32[16,64]{1,0:T(8,128)}, u32[]{:S(2)}) copy-start(f32[16,64]{1,0:T(8,128)} %get-tuple-element.78) | copy-start | bytes 12292
  31.1 14.1 %collective-permute-start.3 = (f32[3,18,1,128]{3,2,1,0:T(1,128)}, f32[3,18,1,128]{3,2,1,0:T(1,128)S(1)}, u32[]{:S(2)}, u32[]{:S(2)}) collective-permute-start(f32[3,18,1,128]{3,2,1,0:T(1,128)} %get-tuple-element.31), channel_id=1, source_target_pairs={{1,0},{2,1},{3,2},{4,3},{5,4},{6,5},{7,6},{8,7},{9,8},{10,9},{11,1... | collective-permute-start | bytes 82952 | tf_op jit(solution)/shard_map/ppermute | solution.py:17
  34.1 11.1 %collective-permute-start.2 = (f32[3,18,1,128]{3,2,1,0:T(1,128)}, f32[3,18,1,128]{3,2,1,0:T(1,128)S(1)}, u32[]{:S(2)}, u32[]{:S(2)}) collective-permute-start(f32[3,18,1,128]{3,2,1,0:T(1,128)} %get-tuple-element.30), channel_id=1, source_target_pairs={{0,1},{1,2},{2,3},{3,4},{4,5},{5,6},{6,7},{7,8},{8,9},{9,10},{10,1... | collective-permute-start | bytes 82952 | tf_op jit(solution)/shard_map/ppermute | solution.py:16
  35.8 8.2 %copy-start.51 = (u32[256]{0:T(256)S(1)}, u32[256]{0:T(256)}, u32[]{:S(2)}) copy-start(u32[256]{0:T(256)} %constant.4) | copy-start | bytes 3076
  55.9 7.2 %collective-permute-start.5 = (f32[3,1,64,128]{3,2,1,0:T(8,128)S(1)}, f32[3,1,64,128]{3,2,1,0:T(8,128)S(1)}, u32[]{:S(2)}, u32[]{:S(2)}) collective-permute-start(f32[3,1,64,128]{3,2,1,0:T(8,128)S(1)} %get-tuple-element.49), channel_id=1, source_target_pairs={{16,0},{32,16},{48,32},{64,48},{80,64},{96,80},{112,96},{128,112},... | collective-permute-start | bytes 294920 | tf_op jit(solution)/shard_map/ppermute | solution.py:17
  60.9 8.2 %collective-permute-start.4 = (f32[3,1,64,128]{3,2,1,0:T(8,128)S(1)}, f32[3,1,64,128]{3,2,1,0:T(8,128)S(1)}, u32[]{:S(2)}, u32[]{:S(2)}) collective-permute-start(f32[3,1,64,128]{3,2,1,0:T(8,128)S(1)} %get-tuple-element.48), channel_id=1, source_target_pairs={{0,16},{16,32},{32,48},{48,64},{64,80},{80,96},{96,112},{112,128},... | collective-permute-start | bytes 294920 | tf_op jit(solution)/shard_map/ppermute | solution.py:16
  69.1 4.7 %collective-permute-start.7 = (f32[3,18,1,128]{3,2,1,0:T(1,128)S(1)}, f32[3,18,1,128]{3,2,1,0:T(1,128)S(1)}, u32[]{:S(2)}, u32[]{:S(2)}) collective-permute-start(f32[3,18,1,128]{3,2,1,0:T(1,128)S(1)} %get-tuple-element.27), channel_id=1, source_target_pairs={{1,0},{2,1},{3,2},{4,3},{5,4},{6,5},{7,6},{8,7},{9,8},{10,9},{11,1... | collective-permute-start | bytes 82952 | tf_op jit(solution)/shard_map/ppermute | solution.py:17
  72.2 5.4 %collective-permute-start.6 = (f32[3,18,1,128]{3,2,1,0:T(1,128)S(1)}, f32[3,18,1,128]{3,2,1,0:T(1,128)S(1)}, u32[]{:S(2)}, u32[]{:S(2)}) collective-permute-start(f32[3,18,1,128]{3,2,1,0:T(1,128)S(1)} %get-tuple-element.26), channel_id=1, source_target_pairs={{0,1},{1,2},{2,3},{3,4},{4,5},{5,6},{6,7},{7,8},{8,9},{9,10},{10,1... | collective-permute-start | bytes 82952 | tf_op jit(solution)/shard_map/ppermute | solution.py:16
  85.4 4.7 %collective-permute-start.9 = (f32[3,1,64,128]{3,2,1,0:T(8,128)S(1)}, f32[3,1,64,128]{3,2,1,0:T(8,128)S(1)}, u32[]{:S(2)}, u32[]{:S(2)}) collective-permute-start(f32[3,1,64,128]{3,2,1,0:T(8,128)S(1)} %get-tuple-element.47), channel_id=1, source_target_pairs={{16,0},{32,16},{48,32},{64,48},{80,64},{96,80},{112,96},{128,112},... | collective-permute-start | bytes 294920 | tf_op jit(solution)/shard_map/ppermute | solution.py:17
  85.5 8.3 %collective-permute-start.8 = (f32[3,1,64,128]{3,2,1,0:T(8,128)S(1)}, f32[3,1,64,128]{3,2,1,0:T(8,128)S(1)}, u32[]{:S(2)}, u32[]{:S(2)}) collective-permute-start(f32[3,1,64,128]{3,2,1,0:T(8,128)S(1)} %get-tuple-element.46), channel_id=1, source_target_pairs={{0,16},{16,32},{32,48},{48,64},{64,80},{80,96},{96,112},{112,128},... | collective-permute-start | bytes 294920 | tf_op jit(solution)/shard_map/ppermute | solution.py:16
  93.9 1.6 collective-permute-start.11
  94.0 5.7 %collective-permute-start.10 = (f32[3,18,1,128]{3,2,1,0:T(1,128)S(1)}, f32[3,18,1,128]{3,2,1,0:T(1,128)S(1)}, u32[]{:S(2)}, u32[]{:S(2)}) collective-permute-start(f32[3,18,1,128]{3,2,1,0:T(1,128)S(1)} %get-tuple-element.22), channel_id=1, source_target_pairs={{0,1},{1,2},{2,3},{3,4},{4,5},{5,6},{6,7},{7,8},{8,9},{9,10},{10,1... | collective-permute-start | bytes 82952 | tf_op jit(solution)/shard_map/ppermute | solution.py:16
  107.5 4.7 %collective-permute-start.13 = (f32[3,1,64,128]{3,2,1,0:T(8,128)S(1)}, f32[3,1,64,128]{3,2,1,0:T(8,128)S(1)}, u32[]{:S(2)}, u32[]{:S(2)}) collective-permute-start(f32[3,1,64,128]{3,2,1,0:T(8,128)S(1)} %get-tuple-element.45), channel_id=1, source_target_pairs={{16,0},{32,16},{48,32},{64,48},{80,64},{96,80},{112,96},{128,112},... | collective-permute-start | bytes 294920 | tf_op jit(solution)/shard_map/ppermute | solution.py:17
  107.6 8.3 %collective-permute-start.12 = (f32[3,1,64,128]{3,2,1,0:T(8,128)S(1)}, f32[3,1,64,128]{3,2,1,0:T(8,128)S(1)}, u32[]{:S(2)}, u32[]{:S(2)}) collective-permute-start(f32[3,1,64,128]{3,2,1,0:T(8,128)S(1)} %get-tuple-element.44), channel_id=1, source_target_pairs={{0,16},{16,32},{32,48},{48,64},{64,80},{80,96},{96,112},{112,128},... | collective-permute-start | bytes 294920 | tf_op jit(solution)/shard_map/ppermute | solution.py:16
  115.9 1.6 collective-permute-start.15
  116.0 5.7 %collective-permute-start.14 = (f32[3,18,1,128]{3,2,1,0:T(1,128)S(1)}, f32[3,18,1,128]{3,2,1,0:T(1,128)S(1)}, u32[]{:S(2)}, u32[]{:S(2)}) collective-permute-start(f32[3,18,1,128]{3,2,1,0:T(1,128)S(1)} %get-tuple-element.18), channel_id=1, source_target_pairs={{0,1},{1,2},{2,3},{3,4},{4,5},{5,6},{6,7},{7,8},{8,9},{9,10},{10,1... | collective-permute-start | bytes 82952 | tf_op jit(solution)/shard_map/ppermute | solution.py:16
  136.6 5.1 %copy-start.18 = (bf16[3072,1,64]{0,2,1:T(8,128)(2,1)S(1)}, bf16[3072,1,64]{0,2,1:T(8,128)(2,1)}, u32[]{:S(2)}) copy-start(bf16[3072,1,64]{0,2,1:T(8,128)(2,1)} %copy.18) | copy-start | bytes 1179652
  (44 other events, 131.1 us)
where the time goes:
time: 268 us
  blocking collectives  125 us (47%)
  other arithmetic  52.6 us (20%)
  local copies, waits for them, and re-layouts  35.8 us (13%)
  waiting for transfers between devices  27.8 us (10%)
  starting transfers between devices  23.9 us (9%)
    unnamed x1, blocking collectives  71.9 us
    psum x1, blocking collectives, body(): spanned = lax.psum(partial_sum, 'gz')  52.9 us
    ppermute x8, waiting for transfers between devices, with_halo(): before = lax.ppermute(last, axis, up)  25.6 us
    add x3, other arithmetic, advance(): return own + total + jnp.stack(mixed, axis=0)  19.4 us
    ppermute x8, starting transfers between devices, with_halo(): after = lax.ppermute(leading, axis, down)  18.9 us
    unnamed x111, local copies, waits for them, and re-layouts  17.3 us
    add x8, other arithmetic, advance(): term = term + weight * own[other_at]  13.3 us
    select_n x2, other arithmetic, lane_weight(): return jnp.where(lower, first[:, :, None], second[:, :, None])  7.98 us
  transfers between devices with their start and end apart: 16, of which 12 were waited for; matrix products, arithmetic and copies ran while one was open for 15% of the time, Pallas kernels for 0%

commit v1 on v0

--- a/solution.py
+++ b/solution.py
@@ -4,6 +4,12 @@
 from jax.sharding import PartitionSpec as P
 
 STEPS = 4
+
+
+def add_all(x, axis):
+    pieces = lax.all_gather(x, axis, axis=0, tiled=False)
+    result = pieces.sum(axis=0)
+    return result
 
 
 def with_halo(x, sides, width):
@@ -76,7 +82,7 @@
     adjoint_flat = adjoint_modes.reshape(-1, 2, modes)
     evolved_flat = evolved.reshape(-1, 2, modes)
     partial_sum = plane_product(adjoint_flat, evolved_flat)
-    spanned = lax.psum(partial_sum, "gz")
+    spanned = add_all(partial_sum, "gz")
     reduced = lax.psum_scatter(spanned, "gx", scatter_dimension=0, tiled=True)
     return (evolved, reduced)
 

time: 268 us -> 234 us (0.87)
  blocking collectives: 125 us -> 89.4 us
    psum x1 -> x0, blocking collectives: 52.9 us -> none  [body(): spanned = lax.psum(partial_sum, 'gz')]
    all_gather x0 -> x1, blocking collectives: none -> 17.5 us  [add_all(): pieces = lax.all_gather(x, axis, axis=0, tiled=False)]
    unnamed x111 -> x110, local copies, waits for them, and re-layouts: 17.3 us -> 17.2 us
  transfers between devices with their start and end apart: 16 -> 16, of which waited for: 12 -> 12; matrix products, arithmetic and copies ran while one was open for 15% -> 17% of each run, Pallas kernels for 0% -> 0%
where the time goes in v1:
time: 234 us; the launch traced here: 232 us
  blocking collectives  89.4 us (38%)
  other arithmetic  52.6 us (22%)
  local copies, waits for them, and re-layouts  35.7 us (15%)
  waiting for transfers between devices  27.8 us (12%)
  starting transfers between devices  23.9 us (10%)
    unnamed x1, blocking collectives  71.9 us
    ppermute x8, waiting for transfers between devices, with_halo(): before = lax.ppermute(last, axis, up)  25.6 us
    add x3, other arithmetic, advance(): return own + total + jnp.stack(mixed, axis=0)  19.4 us
    ppermute x8, starting transfers between devices, with_halo(): after = lax.ppermute(leading, axis, down)  18.9 us
    all_gather x1, blocking collectives, add_all(): pieces = lax.all_gather(x, axis, axis=0, tiled=False)  17.5 us
    unnamed x110, local copies, waits for them, and re-layouts  17.2 us
    add x8, other arithmetic, advance(): term = term + weight * own[other_at]  13.3 us
    select_n x2, other arithmetic, lane_weight(): return jnp.where(lower, first[:, :, None], second[:, :, None])  7.98 us
  transfers between devices with their start and end apart: 16, of which 12 were waited for; matrix products, arithmetic and copies ran while one was open for 17% of the time, Pallas kernels for 0%

profile of v1, /device:TPU:2, one launch (start us, length us, event | category | flops | bytes accessed | tf_op | source)
XLA Modules:
  0.0 232.3 jit_solution(2216094166910237078)
XLA Ops:
  2.2 7.4 %collective-permute-start.1 = (f32[3,1,64,128]{3,2,1,0:T(8,128)}, f32[3,1,64,128]{3,2,1,0:T(8,128)S(1)}, u32[]{:S(2)}, u32[]{:S(2)}) collective-permute-start(f32[3,1,64,128]{3,2,1,0:T(8,128)} %get-tuple-element.45), channel_id=1, source_target_pairs={{16,0},{32,16},{48,32},{64,48},{80,64},{96,80},{112,96},{128,112},... | collective-permute-start | bytes 294920 | tf_op jit(solution)/shard_map/ppermute | solution.py:23
  12.3 3.2 %reshape.118 = bf16[3072,2,64]{2,1,0:T(2,128)(2,1)S(1)} reshape(bf16[3,16,64,128]{3,2,1,0:T(8,128)(2,1)} %param.5) | data formatting | bytes 1572864 | tf_op jit(solution)/shard_map/reshape | solution.py:82
  15.7 3.5 %fusion.172 = (bf16[3072,1,64]{2,1,0:T(2,128)(2,1)}, bf16[3072,1,64]{2,1,0:T(2,128)(2,1)}) fusion(bf16[3072,2,64]{2,1,0:T(2,128)(2,1)S(1)} %reshape.118), kind=kLoop, calls=%fused_computation.399 | loop fusion | bytes 1572864 | tf_op jit(solution)/shard_map/slice | solution.py:67
  19.5 3.9 %broadcast_select_fusion.8 = (f32[16,64,128]{2,1,0:T(8,128)S(1)}, f32[16,64,128]{2,1,0:T(8,128)S(1)}, f32[16,64,128]{2,1,0:T(8,128)S(1)}, f32[16,64,128]{2,1,0:T...) fusion(f32[16,64]{1,0:T(8,128)S(1)} %copy-done.47, ...), kind=kLoop, calls=%fused_computation.316 | loop fusion | flops 1179648 | bytes 4792448 | tf_op jit(solution)/shard_map/jit(_where)/select_n | solution.py:29
  23.4 4.1 %broadcast_select_fusion.17 = (f32[16,64,128]{2,1,0:T(8,128)}, f32[16,64,128]{2,1,0:T(8,128)}, f32[16,64,128]{2,1,0:T(8,128)}, f32[16,64,128]{2,1,0:T(8,128)}, f...) fusion(f32[16,64]{1,0:T(8,128)S(1)} %get-tuple-element.65, ...), kind=kLoop, calls=%fused_computation.325 | loop fusion | flops 1179648 | bytes 4792448 | tf_op jit(solution)/shard_map/jit(_where)/select_n | solution.py:29
  35.8 4.1 %copy.17 = bf16[3072,1,64]{0,2,1:T(8,128)(2,1)} copy(bf16[3072,1,64]{2,1,0:T(2,128)(2,1)} %get-tuple-element.37) | data formatting | bytes 786432
  39.9 4.1 %copy.19 = bf16[3072,1,64]{0,2,1:T(8,128)(2,1)} copy(bf16[3072,1,64]{2,1,0:T(2,128)(2,1)} %get-tuple-element.36) | data formatting | bytes 786432
  49.4 6.4 %fusion.106 = f32[3,16,64,128]{3,2,1,0:T(8,128)S(1)} fusion(f32[3,16,64,128]{3,2,1,0:T(8,128)S(1)} %convert_element_type.6, f32[3,18,66,64]{3,2,1,0:T(8,128)S(1)} %get-tuple-element.9, f32[3,18,66,64]{3,2,1,0:T(8,128)S(1)} %get-tuple-element.8, f32[3,18,65,128]{3,2,1,0:T(8,128)S(1)} %get-tuple-element.23, f32[3,1,64,128]{3,2,1,0:T(8,128)S(1)} %collective-permute-done.1, ...), kind=kLoop, calls=%fused_computation.188 | loop fusion | flops 19660800 | bytes 25614336 | tf_op jit(solution)/shard_map/add | solution.py:60
  55.9 5.0 %collective-permute-start.5 = (f32[3,1,64,128]{3,2,1,0:T(8,128)S(1)}, f32[3,1,64,128]{3,2,1,0:T(8,128)S(1)}, u32[]{:S(2)}, u32[]{:S(2)}) collective-permute-start(f32[3,1,64,128]{3,2,1,0:T(8,128)S(1)} %get-tuple-element.43), channel_id=1, source_target_pairs={{16,0},{32,16},{48,32},{64,48},{80,64},{96,80},{112,96},{128,112},... | collective-permute-start | bytes 294920 | tf_op jit(solution)/shard_map/ppermute | solution.py:23
  63.1 6.0 %collective-permute-done.4 = f32[3,1,64,128]{3,2,1,0:T(8,128)S(1)} collective-permute-done((f32[3,1,64,128]{3,2,1,0:T(8,128)S(1)}, f32[3,1,64,128]{3,2,1,0:T(8,128)S(1)}, u32[]{:S(2)}, u32[]{:S(2)}) %collective-permute-start.4) | collective-permute-done | bytes 98336 | tf_op jit(solution)/shard_map/ppermute | solution.py:22
  69.1 3.1 %collective-permute-start.7 = (f32[3,18,1,128]{3,2,1,0:T(1,128)S(1)}, f32[3,18,1,128]{3,2,1,0:T(1,128)S(1)}, u32[]{:S(2)}, u32[]{:S(2)}) collective-permute-start(f32[3,18,1,128]{3,2,1,0:T(1,128)S(1)} %get-tuple-element.21), channel_id=1, source_target_pairs={{1,0},{2,1},{3,2},{4,3},{5,4},{6,5},{7,6},{8,7},{9,8},{10,9},{11,1... | collective-permute-start | bytes 82952 | tf_op jit(solution)/shard_map/ppermute | solution.py:23
  73.8 3.8 %collective-permute-done.6 = f32[3,18,1,128]{3,2,1,0:T(1,128)S(1)} collective-permute-done((f32[3,18,1,128]{3,2,1,0:T(1,128)S(1)}, f32[3,18,1,128]{3,2,1,0:T(1,128)S(1)}, u32[]{:S(2)}, u32[]{:S(2)}) %collective-permute-start.6) | collective-permute-done | bytes 27680 | tf_op jit(solution)/shard_map/ppermute | solution.py:22
  78.9 6.5 %fusion.72 = f32[3,16,64,128]{3,2,1,0:T(8,128)S(1)} fusion(f32[3,16,64,128]{3,2,1,0:T(8,128)S(1)} %fusion.106, f32[3,18,66,64]{3,2,1,0:T(8,128)S(1)} %get-tuple-element.7, f32[3,18,66,64]{3,2,1,0:T(8,128)S(1)} %get-tuple-element.6, f32[3,18,65,128]{3,2,1,0:T(8,128)S(1)} %get-tuple-element.19, f32[3,1,64,128]{3,2,1,0:T(8,128)S(1)} %collective-permute-done.5, ...), kind=kLoop, calls=%fused_computation.131 | loop fusion | flops 19660800 | bytes 25614336 | tf_op jit(solution)/shard_map/add | solution.py:60
  90.1 3.7 %collective-permute-done.8 = f32[3,1,64,128]{3,2,1,0:T(8,128)S(1)} collective-permute-done((f32[3,1,64,128]{3,2,1,0:T(8,128)S(1)}, f32[3,1,64,128]{3,2,1,0:T(8,128)S(1)}, u32[]{:S(2)}, u32[]{:S(2)}) %collective-permute-start.8) | collective-permute-done | bytes 98336 | tf_op jit(solution)/shard_map/ppermute | solution.py:22
  95.5 4.1 %collective-permute-done.10 = f32[3,18,1,128]{3,2,1,0:T(1,128)S(1)} collective-permute-done((f32[3,18,1,128]{3,2,1,0:T(1,128)S(1)}, f32[3,18,1,128]{3,2,1,0:T(1,128)S(1)}, u32[]{:S(2)}, u32[]{:S(2)}) %collective-permute-start.10) | collective-permute-done | bytes 27680 | tf_op jit(solution)/shard_map/ppermute | solution.py:22
  101.0 6.5 %fusion.38 = f32[3,16,64,128]{3,2,1,0:T(8,128)S(1)} fusion(f32[3,16,64,128]{3,2,1,0:T(8,128)S(1)} %fusion.72, f32[3,18,66,64]{3,2,1,0:T(8,128)S(1)} %get-tuple-element.5, f32[3,18,66,64]{3,2,1,0:T(8,128)S(1)} %get-tuple-element.4, f32[3,18,65,128]{3,2,1,0:T(8,128)S(1)} %get-tuple-element.15, f32[3,1,64,128]{3,2,1,0:T(8,128)S(1)} %collective-permute-done.9, ...), kind=kLoop, calls=%fused_computation.74 | loop fusion | flops 19660800 | bytes 25614336 | tf_op jit(solution)/shard_map/add | solution.py:60
  112.2 3.7 %collective-permute-done.12 = f32[3,1,64,128]{3,2,1,0:T(8,128)S(1)} collective-permute-done((f32[3,1,64,128]{3,2,1,0:T(8,128)S(1)}, f32[3,1,64,128]{3,2,1,0:T(8,128)S(1)}, u32[]{:S(2)}, u32[]{:S(2)}) %collective-permute-start.12) | collective-permute-done | bytes 98336 | tf_op jit(solution)/shard_map/ppermute | solution.py:22
  117.5 4.2 %collective-permute-done.14 = f32[3,18,1,128]{3,2,1,0:T(1,128)S(1)} collective-permute-done((f32[3,18,1,128]{3,2,1,0:T(1,128)S(1)}, f32[3,18,1,128]{3,2,1,0:T(1,128)S(1)}, u32[]{:S(2)}, u32[]{:S(2)}) %collective-permute-start.14) | collective-permute-done | bytes 27680 | tf_op jit(solution)/shard_map/ppermute | solution.py:22
  123.0 7.3 %fusion.4 = bf16[3,16,64,128]{3,2,1,0:T(8,128)(2,1)} fusion(f32[3,16,64,128]{3,2,1,0:T(8,128)S(1)} %fusion.38, f32[3,18,66,64]{3,2,1,0:T(8,128)S(1)} %get-tuple-element.3, f32[3,18,66,64]{3,2,1,0:T(8,128)S(1)} %get-tuple-element.2, f32[3,18,65,128]{3,2,1,0:T(8,128)S(1)} %get-tuple-element.11, f32[3,1,64,128]{3,2,1,0:T(8,128)S(1)} %collective-permute-done.13, ...), kind=kLoop, calls=%fused_computation.17 | loop fusion | flops 20054016 | bytes 24827904 | tf_op jit(solution)/shard_map/convert_element_type | solution.py:81
  130.3 3.2 %reshape.117 = bf16[3072,2,64]{2,1,0:T(2,128)(2,1)S(1)} reshape(bf16[3,16,64,128]{3,2,1,0:T(8,128)(2,1)} %fusion.4) | data formatting | bytes 1572864 | tf_op jit(solution)/shard_map/reshape | solution.py:83
  133.5 3.1 %fusion.171 = (bf16[3072,1,64]{2,1,0:T(2,128)(2,1)S(1)}, bf16[3072,1,64]{2,1,0:T(2,128)(2,1)}) fusion(bf16[3072,2,64]{2,1,0:T(2,128)(2,1)S(1)} %reshape.117), kind=kLoop, calls=%fused_computation.398 | loop fusion | bytes 1572864 | tf_op jit(solution)/shard_map/slice | solution.py:68
  136.6 3.5 %copy.16 = bf16[3072,1,64]{0,2,1:T(8,128)(2,1)S(1)} copy(bf16[3072,1,64]{2,1,0:T(2,128)(2,1)} %get-tuple-element.35) | data formatting | bytes 786432
  142.2 17.5 %all-gather = f32[1024,64]{1,0:T(8,128)S(1)} all-gather(f32[64,64]{1,0:T(8,128)S(1)} %copy.10), channel_id=2, replica_groups=mesh['gx'=16,'gz'=16] {'gz'}, dimensions={0}, use_global_device_ids=true | all-gather | bytes 278528 | tf_op jit(solution)/shard_map/all_gather | solution.py:10
  159.8 71.9 %all-reduce = f32[64,64]{1,0:T(8,128)S(1)} all-reduce(f32[64,64]{1,0:T(8,128)S(1)} %reduce_sum.9), channel_id=3, replica_groups=mesh['gx'=16,'gz'=16] {'gx'}, use_global_device_ids=true, to_apply=%region_1.2.clone | all-reduce | flops 4096 | bytes 32768
  (167 shorter events, 40.2 us)
Async XLA Ops:
  0.6 10.3 %copy-start.20 = (f32[36,16,64]{2,1,0:T(8,128)S(1)}, f32[36,16,64]{2,1,0:T(8,128)}, u32[]{:S(2)}) copy-start(f32[36,16,64]{2,1,0:T(8,128)} %param.6) | copy-start | bytes 442372
  2.2 10.1 %copy-start.21 = (f32[18,16,64]{2,1,0:T(8,128)S(1)}, f32[18,16,64]{2,1,0:T(8,128)}, u32[]{:S(2)}) copy-start(f32[18,16,64]{2,1,0:T(8,128)} %param.7) | copy-start | bytes 221188
  2.2 28.2 %collective-permute-start.1 = (f32[3,1,64,128]{3,2,1,0:T(8,128)}, f32[3,1,64,128]{3,2,1,0:T(8,128)S(1)}, u32[]{:S(2)}, u32[]{:S(2)}) collective-permute-start(f32[3,1,64,128]{3,2,1,0:T(8,128)} %get-tuple-element.45), channel_id=1, source_target_pairs={{16,0},{32,16},{48,32},{64,48},{80,64},{96,80},{112,96},{128,112},... | collective-permute-start | bytes 294920 | tf_op jit(solution)/shard_map/ppermute | solution.py:23
  9.6 20.8 %collective-permute-start = (f32[3,1,64,128]{3,2,1,0:T(8,128)}, f32[3,1,64,128]{3,2,1,0:T(8,128)S(1)}, u32[]{:S(2)}, u32[]{:S(2)}) collective-permute-start(f32[3,1,64,128]{3,2,1,0:T(8,128)} %get-tuple-element.44), channel_id=1, source_target_pairs={{0,16},{16,32},{32,48},{48,64},{64,80},{80,96},{96,112},{112,128},... | collective-permute-start | bytes 294920 | tf_op jit(solution)/shard_map/ppermute | solution.py:22
  19.4 4.0 %copy-start.22 = (f32[16,64]{1,0:T(8,128)S(1)}, f32[16,64]{1,0:T(8,128)}, u32[]{:S(2)}) copy-start(f32[16,64]{1,0:T(8,128)} %get-tuple-element.69) | copy-start | bytes 12292
  19.4 4.0 %copy-start.23 = (f32[16,64]{1,0:T(8,128)S(1)}, f32[16,64]{1,0:T(8,128)}, u32[]{:S(2)}) copy-start(f32[16,64]{1,0:T(8,128)} %get-tuple-element.70) | copy-start | bytes 12292
  19.4 4.0 %copy-start.24 = (f32[16,64]{1,0:T(8,128)S(1)}, f32[16,64]{1,0:T(8,128)}, u32[]{:S(2)}) copy-start(f32[16,64]{1,0:T(8,128)} %get-tuple-element.71) | copy-start | bytes 12292
  19.4 4.0 %copy-start.25 = (f32[16,64]{1,0:T(8,128)S(1)}, f32[16,64]{1,0:T(8,128)}, u32[]{:S(2)}) copy-start(f32[16,64]{1,0:T(8,128)} %get-tuple-element.72) | copy-start | bytes 12292
  31.1 14.1 %collective-permute-start.3 = (f32[3,18,1,128]{3,2,1,0:T(1,128)}, f32[3,18,1,128]{3,2,1,0:T(1,128)S(1)}, u32[]{:S(2)}, u32[]{:S(2)}) collective-permute-start(f32[3,18,1,128]{3,2,1,0:T(1,128)} %get-tuple-element.25), channel_id=1, source_target_pairs={{1,0},{2,1},{3,2},{4,3},{5,4},{6,5},{7,6},{8,7},{9,8},{10,9},{11,1... | collective-permute-start | bytes 82952 | tf_op jit(solution)/shard_map/ppermute | solution.py:23
  34.1 11.1 %collective-permute-start.2 = (f32[3,18,1,128]{3,2,1,0:T(1,128)}, f32[3,18,1,128]{3,2,1,0:T(1,128)S(1)}, u32[]{:S(2)}, u32[]{:S(2)}) collective-permute-start(f32[3,18,1,128]{3,2,1,0:T(1,128)} %get-tuple-element.24), channel_id=1, source_target_pairs={{0,1},{1,2},{2,3},{3,4},{4,5},{5,6},{6,7},{7,8},{8,9},{9,10},{10,1... | collective-permute-start | bytes 82952 | tf_op jit(solution)/shard_map/ppermute | solution.py:22
  35.8 8.2 %copy-start.51 = (u32[256]{0:T(256)S(1)}, u32[256]{0:T(256)}, u32[]{:S(2)}) copy-start(u32[256]{0:T(256)} %constant.6) | copy-start | bytes 3076
  55.9 7.2 %collective-permute-start.5 = (f32[3,1,64,128]{3,2,1,0:T(8,128)S(1)}, f32[3,1,64,128]{3,2,1,0:T(8,128)S(1)}, u32[]{:S(2)}, u32[]{:S(2)}) collective-permute-start(f32[3,1,64,128]{3,2,1,0:T(8,128)S(1)} %get-tuple-element.43), channel_id=1, source_target_pairs={{16,0},{32,16},{48,32},{64,48},{80,64},{96,80},{112,96},{128,112},... | collective-permute-start | bytes 294920 | tf_op jit(solution)/shard_map/ppermute | solution.py:23
  60.9 8.2 %collective-permute-start.4 = (f32[3,1,64,128]{3,2,1,0:T(8,128)S(1)}, f32[3,1,64,128]{3,2,1,0:T(8,128)S(1)}, u32[]{:S(2)}, u32[]{:S(2)}) collective-permute-start(f32[3,1,64,128]{3,2,1,0:T(8,128)S(1)} %get-tuple-element.42), channel_id=1, source_target_pairs={{0,16},{16,32},{32,48},{48,64},{64,80},{80,96},{96,112},{112,128},... | collective-permute-start | bytes 294920 | tf_op jit(solution)/shard_map/ppermute | solution.py:22
  69.1 4.7 %collective-permute-start.7 = (f32[3,18,1,128]{3,2,1,0:T(1,128)S(1)}, f32[3,18,1,128]{3,2,1,0:T(1,128)S(1)}, u32[]{:S(2)}, u32[]{:S(2)}) collective-permute-start(f32[3,18,1,128]{3,2,1,0:T(1,128)S(1)} %get-tuple-element.21), channel_id=1, source_target_pairs={{1,0},{2,1},{3,2},{4,3},{5,4},{6,5},{7,6},{8,7},{9,8},{10,9},{11,1... | collective-permute-start | bytes 82952 | tf_op jit(solution)/shard_map/ppermute | solution.py:23
  72.2 5.4 %collective-permute-start.6 = (f32[3,18,1,128]{3,2,1,0:T(1,128)S(1)}, f32[3,18,1,128]{3,2,1,0:T(1,128)S(1)}, u32[]{:S(2)}, u32[]{:S(2)}) collective-permute-start(f32[3,18,1,128]{3,2,1,0:T(1,128)S(1)} %get-tuple-element.20), channel_id=1, source_target_pairs={{0,1},{1,2},{2,3},{3,4},{4,5},{5,6},{6,7},{7,8},{8,9},{9,10},{10,1... | collective-permute-start | bytes 82952 | tf_op jit(solution)/shard_map/ppermute | solution.py:22
  85.4 4.7 %collective-permute-start.9 = (f32[3,1,64,128]{3,2,1,0:T(8,128)S(1)}, f32[3,1,64,128]{3,2,1,0:T(8,128)S(1)}, u32[]{:S(2)}, u32[]{:S(2)}) collective-permute-start(f32[3,1,64,128]{3,2,1,0:T(8,128)S(1)} %get-tuple-element.41), channel_id=1, source_target_pairs={{16,0},{32,16},{48,32},{64,48},{80,64},{96,80},{112,96},{128,112},... | collective-permute-start | bytes 294920 | tf_op jit(solution)/shard_map/ppermute | solution.py:23
  85.5 8.3 %collective-permute-start.8 = (f32[3,1,64,128]{3,2,1,0:T(8,128)S(1)}, f32[3,1,64,128]{3,2,1,0:T(8,128)S(1)}, u32[]{:S(2)}, u32[]{:S(2)}) collective-permute-start(f32[3,1,64,128]{3,2,1,0:T(8,128)S(1)} %get-tuple-element.40), channel_id=1, source_target_pairs={{0,16},{16,32},{32,48},{48,64},{64,80},{80,96},{96,112},{112,128},... | collective-permute-start | bytes 294920 | tf_op jit(solution)/shard_map/ppermute | solution.py:22
  93.9 1.6 collective-permute-start.11
  94.0 5.7 %collective-permute-start.10 = (f32[3,18,1,128]{3,2,1,0:T(1,128)S(1)}, f32[3,18,1,128]{3,2,1,0:T(1,128)S(1)}, u32[]{:S(2)}, u32[]{:S(2)}) collective-permute-start(f32[3,18,1,128]{3,2,1,0:T(1,128)S(1)} %get-tuple-element.16), channel_id=1, source_target_pairs={{0,1},{1,2},{2,3},{3,4},{4,5},{5,6},{6,7},{7,8},{8,9},{9,10},{10,1... | collective-permute-start | bytes 82952 | tf_op jit(solution)/shard_map/ppermute | solution.py:22
  107.5 4.7 %collective-permute-start.13 = (f32[3,1,64,128]{3,2,1,0:T(8,128)S(1)}, f32[3,1,64,128]{3,2,1,0:T(8,128)S(1)}, u32[]{:S(2)}, u32[]{:S(2)}) collective-permute-start(f32[3,1,64,128]{3,2,1,0:T(8,128)S(1)} %get-tuple-element.39), channel_id=1, source_target_pairs={{16,0},{32,16},{48,32},{64,48},{80,64},{96,80},{112,96},{128,112},... | collective-permute-start | bytes 294920 | tf_op jit(solution)/shard_map/ppermute | solution.py:23
  107.6 8.3 %collective-permute-start.12 = (f32[3,1,64,128]{3,2,1,0:T(8,128)S(1)}, f32[3,1,64,128]{3,2,1,0:T(8,128)S(1)}, u32[]{:S(2)}, u32[]{:S(2)}) collective-permute-start(f32[3,1,64,128]{3,2,1,0:T(8,128)S(1)} %get-tuple-element.38), channel_id=1, source_target_pairs={{0,16},{16,32},{32,48},{48,64},{64,80},{80,96},{96,112},{112,128},... | collective-permute-start | bytes 294920 | tf_op jit(solution)/shard_map/ppermute | solution.py:22
  115.9 1.6 collective-permute-start.15
  116.0 5.7 %collective-permute-start.14 = (f32[3,18,1,128]{3,2,1,0:T(1,128)S(1)}, f32[3,18,1,128]{3,2,1,0:T(1,128)S(1)}, u32[]{:S(2)}, u32[]{:S(2)}) collective-permute-start(f32[3,18,1,128]{3,2,1,0:T(1,128)S(1)} %get-tuple-element.12), channel_id=1, source_target_pairs={{0,1},{1,2},{2,3},{3,4},{4,5},{5,6},{6,7},{7,8},{8,9},{9,10},{10,1... | collective-permute-start | bytes 82952 | tf_op jit(solution)/shard_map/ppermute | solution.py:22
  136.6 5.1 %copy-start.18 = (bf16[3072,1,64]{0,2,1:T(8,128)(2,1)S(1)}, bf16[3072,1,64]{0,2,1:T(8,128)(2,1)}, u32[]{:S(2)}) copy-start(bf16[3072,1,64]{0,2,1:T(8,128)(2,1)} %copy.17) | copy-start | bytes 1179652
  (44 other events, 131.1 us)
